TPU v7x, 32 devices: a whole 2x2x4 slice. The times are simulated.
32 devices in a mesh: dp: 8 (over y, x, core), tensor: 4 (over z).
Axes of the slice: x: 2, y: 2, z: 4, core: 2. Of those that a mesh axis runs over, the one named last changes fastest.
Arguments:
- block_input: bfloat16 [2, 512, 16, 1536], P(None, 'tensor', 'dp'), may hold values from -6 to 6
- lengths: int32 [2, 16, 3], P(None, 'dp'), may hold values from 64 to 320, as said below
- out_grad: bfloat16 [2, 512, 16, 1536], P(None, 'tensor', 'dp'), may hold values from -6 to 6
- w_query: bfloat16 [1536, 1536], P('dp', 'tensor'), may hold values from -0.15625 to 0.15625
- w_key: bfloat16 [1536, 1536], P('dp', 'tensor'), may hold values from -0.15625 to 0.15625
- w_value: bfloat16 [1536, 1536], P('dp', 'tensor'), may hold values from -0.15625 to 0.15625
- w_out: bfloat16 [1536, 1536], P('tensor', 'dp'), may hold values from -1.75 to 1.75
- w_gate: bfloat16 [1536, 4096], P('dp', 'tensor'), may hold values from -0.15625 to 0.15625
- w_up: bfloat16 [1536, 4096], P('dp', 'tensor'), may hold values from -0.15625 to 0.15625
- w_down: bfloat16 [4096, 1536], P('tensor', 'dp'), may hold values from -0.1875 to 0.1875
- attn_gain: bfloat16 [1536], P('dp'), may hold values from 0.5 to 1.5
- ffn_gain: bfloat16 [1536], P('dp'), may hold values from 0.5 to 1.5
Outputs:
- block_output: bfloat16 [2, 512, 16, 1536], P(None, 'tensor', 'dp')
- input_grad: bfloat16 [2, 512, 16, 1536], P(None, 'tensor', 'dp')
- grad_query: float32 [1536, 1536], P('dp', 'tensor')
- grad_key: float32 [1536, 1536], P('dp', 'tensor')
- grad_value: float32 [1536, 1536], P('dp', 'tensor')
- grad_out: float32 [1536, 1536], P('tensor', 'dp')
- grad_gate: float32 [1536, 4096], P('dp', 'tensor')
- grad_up: float32 [1536, 4096], P('dp', 'tensor')
- grad_down: float32 [4096, 1536], P('tensor', 'dp')
- grad_attn_gain: float32 [1536], P('dp')
- grad_ffn_gain: float32 [1536], P('dp')
Inputs may be any that keep to these rules, and one draw needn't show every extreme that they name: Each group's 512 slots hold, in order, its prompt of lengths[..., 0] tokens and two continuations of lengths[..., 1] and lengths[..., 2] tokens; the three sum to 512; a prompt has 192 tokens or more.
All inputs are finite; a program needn't handle non-finite values.
Results may differ from a plain program's by a relative error of at most 0.023.
Values may be sent and summed in bfloat16 or wider, within the bound.
A program may use at most 192 MiB of HBM per device.

v0:
```python
import math

import jax
import jax.numpy as jnp
from jax import lax
from jax.sharding import PartitionSpec as P

HD = 64
GTOK = 512


EPSILON = 1e-05
MASKED = -1e30


def layout_tables(group_lengths):
    slot_index = jnp.arange(GTOK, dtype=jnp.int32)[:, None]
    prompt_len = group_lengths[:, 0][None, :]
    first_len = group_lengths[:, 1][None, :]
    segment = jnp.where(
        slot_index < prompt_len, 0, jnp.where(slot_index < prompt_len + first_len, 1, 2)
    ).astype(jnp.int32)
    position = jnp.where(segment == 2, slot_index - first_len, slot_index)
    frequency = jnp.exp(jnp.arange(HD // 2, dtype=jnp.float32) * (-2.0 * math.log(10000.0) / HD))
    angles = position.astype(jnp.float32)[:, :, None] * frequency
    return (segment, jnp.cos(angles), jnp.sin(angles))


def rotate(values, cos_table, sin_table):
    half_size = values.shape[-1] // 2
    first_half = values[..., :half_size]
    second_half = values[..., half_size:]
    cos_wide = cos_table[:, :, None, :]
    sin_wide = sin_table[:, :, None, :]
    return jnp.concatenate(
        [
            first_half * cos_wide - second_half * sin_wide,
            second_half * cos_wide + first_half * sin_wide,
        ],
        axis=-1,
    )


def rotate_back(values, cos_table, sin_table):
    half_size = values.shape[-1] // 2
    first_half = values[..., :half_size]
    second_half = values[..., half_size:]
    cos_wide = cos_table[:, :, None, :]
    sin_wide = sin_table[:, :, None, :]
    return jnp.concatenate(
        [
            first_half * cos_wide + second_half * sin_wide,
            second_half * cos_wide - first_half * sin_wide,
        ],
        axis=-1,
    )


def rms_scale(values):
    return lax.rsqrt(jnp.mean(values * values, axis=-1, keepdims=True) + EPSILON)


def norm_back(upstream, unit_rows, gain_row, scale_rows):
    scaled = upstream * gain_row
    return scale_rows * (scaled - unit_rows * jnp.mean(scaled * unit_rows, axis=-1, keepdims=True))


def attention_scores(queries, key_rows, allowed):
    scores = jnp.einsum(
        "tghe,sghe->ghts", queries, key_rows, preferred_element_type=jnp.float32
    ) * HD ** (-0.5)
    return jnp.where(allowed[:, None], scores, MASKED)


def add_tuples(first_set, second_set):
    return tuple((earlier + later for earlier, later in zip(first_set, second_set)))


def micro_step(inputs, group_lengths, upstream, gathered):
    w_query, w_key, w_value, w_out, w_gate, w_up, w_down, attn_gain, ffn_gain = gathered
    gain_one = attn_gain.astype(jnp.float32)
    gain_two = ffn_gain.astype(jnp.float32)
    group_count = inputs.shape[1]
    head_cols = w_query.shape[1]
    hidden_cols = w_gate.shape[1]
    shape_heads = (GTOK, group_count, head_cols // HD, HD)
    segment, cos_table, sin_table = layout_tables(group_lengths)
    token_index = jnp.arange(GTOK, dtype=jnp.int32)
    seg_groups = segment.T
    allowed = (token_index[None, None, :] <= token_index[None, :, None]) & (
        (seg_groups[:, None, :] == 0) | (seg_groups[:, None, :] == seg_groups[:, :, None])
    )
    residual = inputs.astype(jnp.float32)
    scale_one = rms_scale(residual)
    unit_one = residual * scale_one
    normed_one = (unit_one * gain_one).astype(jnp.bfloat16)
    normed_all = lax.all_gather(normed_one, "tensor", axis=0, tiled=True)
    w_joint = jnp.concatenate([w_query, w_key, w_value], axis=1)
    projected = jnp.einsum("tgd,dc->tgc", normed_all, w_joint, preferred_element_type=jnp.float32)
    queries = rotate(projected[..., :head_cols].reshape(shape_heads), cos_table, sin_table).astype(
        jnp.bfloat16
    )
    key_rows = rotate(
        projected[..., head_cols : 2 * head_cols].reshape(shape_heads), cos_table, sin_table
    ).astype(jnp.bfloat16)
    value_rows = projected[..., 2 * head_cols :].reshape(shape_heads).astype(jnp.bfloat16)
    scores = attention_scores(queries, key_rows, allowed)
    row_max = jnp.max(scores, axis=-1, keepdims=True)
    log_total = row_max + jnp.log(jnp.sum(jnp.exp(scores - row_max), axis=-1, keepdims=True))
    attn_probs = jnp.exp(scores - log_total).astype(jnp.bfloat16)
    attn_mix = (
        jnp.einsum("ghts,sghe->tghe", attn_probs, value_rows, preferred_element_type=jnp.float32)
        .astype(jnp.bfloat16)
        .reshape(GTOK, group_count, head_cols)
    )
    rows_here = attn_mix
    attn_sum = lax.psum_scatter(
        jnp.einsum("tgc,cd->tgd", rows_here, w_out, preferred_element_type=jnp.float32),
        "tensor",
        scatter_dimension=0,
        tiled=True,
    )
    middle = residual + attn_sum
    scale_two = rms_scale(middle)
    unit_two = middle * scale_two
    normed_two = (unit_two * gain_two).astype(jnp.bfloat16)
    normed_more = lax.all_gather(normed_two, "tensor", axis=0, tiled=True)
    w_gate_up = jnp.concatenate([w_gate, w_up], axis=1)
    gate_up = jnp.einsum("tgd,df->tgf", normed_more, w_gate_up, preferred_element_type=jnp.float32)
    gate_vals = gate_up[..., :hidden_cols]
    up_vals = gate_up[..., hidden_cols:]
    sigmoid_gate = jax.nn.sigmoid(gate_vals)
    silu_gate = gate_vals * sigmoid_gate
    hidden = (silu_gate * up_vals).astype(jnp.bfloat16)
    rows_here = hidden
    ffn_sum = lax.psum_scatter(
        jnp.einsum("tgf,fd->tgd", rows_here, w_down, preferred_element_type=jnp.float32).astype(
            jnp.bfloat16
        ),
        "tensor",
        scatter_dimension=0,
        tiled=True,
    ).astype(jnp.float32)
    output = (middle + ffn_sum).astype(jnp.bfloat16)
    upstream_all = lax.all_gather(upstream, "tensor", axis=0, tiled=True)
    hidden_grad = jnp.einsum(
        "tgd,fd->tgf", upstream_all, w_down, preferred_element_type=jnp.float32
    )
    grad_down = jnp.einsum("tgf,tgd->fd", hidden, upstream_all, preferred_element_type=jnp.float32)
    up_grad = hidden_grad * silu_gate
    gate_grad = hidden_grad * up_vals * (sigmoid_gate * (1.0 + gate_vals * (1.0 - sigmoid_gate)))
    gate_up_grad = jnp.concatenate([gate_grad, up_grad], axis=-1).astype(jnp.bfloat16)
    grad_gate_up = jnp.einsum(
        "tgd,tgf->df", normed_more, gate_up_grad, preferred_element_type=jnp.float32
    )
    rows_here = gate_up_grad
    normed_two_grad = lax.psum_scatter(
        jnp.einsum("tgf,df->tgd", rows_here, w_gate_up, preferred_element_type=jnp.float32).astype(
            jnp.bfloat16
        ),
        "tensor",
        scatter_dimension=0,
        tiled=True,
    ).astype(jnp.float32)
    gain_two_grad = jnp.sum(normed_two_grad * unit_two, axis=(0, 1))
    middle_grad = upstream.astype(jnp.float32) + norm_back(
        normed_two_grad, unit_two, gain_two, scale_two
    )
    attn_grad = middle_grad.astype(jnp.bfloat16)
    attn_grad_all = lax.all_gather(attn_grad, "tensor", axis=0, tiled=True)
    mix_grad = (
        jnp.einsum("tgd,cd->tgc", attn_grad_all, w_out, preferred_element_type=jnp.float32)
        .astype(jnp.bfloat16)
        .reshape(shape_heads)
    )
    grad_out = jnp.einsum(
        "tgc,tgd->cd", attn_mix, attn_grad_all, preferred_element_type=jnp.float32
    )
    scores_again = attention_scores(queries, key_rows, allowed)
    probs_full = jnp.exp(scores_again - log_total)
    prob_grad = jnp.einsum(
        "tghe,sghe->ghts", mix_grad, value_rows, preferred_element_type=jnp.float32
    )
    value_grad = jnp.einsum(
        "ghts,tghe->sghe",
        probs_full.astype(jnp.bfloat16),
        mix_grad,
        preferred_element_type=jnp.float32,
    )
    centre = jnp.sum(probs_full * prob_grad, axis=-1, keepdims=True)
    score_grad = (probs_full * (prob_grad - centre)).astype(jnp.bfloat16)
    query_grad = jnp.einsum(
        "ghts,sghe->tghe", score_grad, key_rows, preferred_element_type=jnp.float32
    ) * HD ** (-0.5)
    key_grad = jnp.einsum(
        "ghts,tghe->sghe", score_grad, queries, preferred_element_type=jnp.float32
    ) * HD ** (-0.5)
    flat_shape = (GTOK, group_count, head_cols)
    joint_grad = jnp.concatenate(
        [
            rotate_back(query_grad, cos_table, sin_table).reshape(flat_shape),
            rotate_back(key_grad, cos_table, sin_table).reshape(flat_shape),
            value_grad.reshape(flat_shape),
        ],
        axis=-1,
    ).astype(jnp.bfloat16)
    grad_joint = jnp.einsum(
        "tgd,tgc->dc", normed_all, joint_grad, preferred_element_type=jnp.float32
    )
    rows_here = joint_grad
    normed_one_grad = lax.psum_scatter(
        jnp.einsum("tgc,dc->tgd", rows_here, w_joint, preferred_element_type=jnp.float32).astype(
            jnp.bfloat16
        ),
        "tensor",
        scatter_dimension=0,
        tiled=True,
    ).astype(jnp.float32)
    gain_one_grad = jnp.sum(normed_one_grad * unit_one, axis=(0, 1))
    input_grad = (middle_grad + norm_back(normed_one_grad, unit_one, gain_one, scale_one)).astype(
        jnp.bfloat16
    )
    param_grads = (
        grad_joint[:, :head_cols],
        grad_joint[:, head_cols : 2 * head_cols],
        grad_joint[:, 2 * head_cols :],
        grad_out,
        grad_gate_up[:, :hidden_cols],
        grad_gate_up[:, hidden_cols:],
        grad_down,
        gain_one_grad,
        gain_two_grad,
    )
    return (output, input_grad, param_grads)


def body(
    block_input,
    lengths,
    out_grad,
    w_query,
    w_key,
    w_value,
    w_out,
    w_gate,
    w_up,
    w_down,
    attn_gain,
    ffn_gain,
):
    outputs = []
    input_grads = []
    totals = None
    shares = None
    for micro_index in range(block_input.shape[0]):
        gathered = (
            lax.all_gather(w_query, "dp", axis=0, tiled=True),
            lax.all_gather(w_key, "dp", axis=0, tiled=True),
            lax.all_gather(w_value, "dp", axis=0, tiled=True),
            lax.all_gather(w_out, "dp", axis=1, tiled=True),
            lax.all_gather(w_gate, "dp", axis=0, tiled=True),
            lax.all_gather(w_up, "dp", axis=0, tiled=True),
            lax.all_gather(w_down, "dp", axis=1, tiled=True),
            lax.all_gather(attn_gain, "dp", axis=0, tiled=True),
            lax.all_gather(ffn_gain, "dp", axis=0, tiled=True),
        )
        output, input_grad, param_grads = micro_step(
            block_input[micro_index], lengths[micro_index], out_grad[micro_index], gathered
        )
        outputs.append(output)
        input_grads.append(input_grad)
        totals = param_grads if totals is None else add_tuples(totals, param_grads)
    shares = (
        lax.psum_scatter(
            totals[0].astype(jnp.bfloat16), "dp", scatter_dimension=0, tiled=True
        ).astype(jnp.float32),
        lax.psum_scatter(
            totals[1].astype(jnp.bfloat16), "dp", scatter_dimension=0, tiled=True
        ).astype(jnp.float32),
        lax.psum_scatter(
            totals[2].astype(jnp.bfloat16), "dp", scatter_dimension=0, tiled=True
        ).astype(jnp.float32),
        lax.psum_scatter(
            totals[3].astype(jnp.bfloat16), "dp", scatter_dimension=1, tiled=True
        ).astype(jnp.float32),
        lax.psum_scatter(
            totals[4].astype(jnp.bfloat16), "dp", scatter_dimension=0, tiled=True
        ).astype(jnp.float32),
        lax.psum_scatter(
            totals[5].astype(jnp.bfloat16), "dp", scatter_dimension=0, tiled=True
        ).astype(jnp.float32),
        lax.psum_scatter(
            totals[6].astype(jnp.bfloat16), "dp", scatter_dimension=1, tiled=True
        ).astype(jnp.float32),
        lax.psum_scatter(
            totals[7].astype(jnp.bfloat16), "dp", scatter_dimension=0, tiled=True
        ).astype(jnp.float32),
        lax.psum_scatter(
            totals[8].astype(jnp.bfloat16), "dp", scatter_dimension=0, tiled=True
        ).astype(jnp.float32),
    )
    gain_one_total, gain_two_total = lax.psum((shares[7], shares[8]), "tensor")
    return (
        jnp.stack(outputs),
        jnp.stack(input_grads),
        shares[0],
        shares[1],
        shares[2],
        shares[3],
        shares[4],
        shares[5],
        shares[6],
        gain_one_total,
        gain_two_total,
    )


def solution(mesh):
    placed = (
        P(None, "tensor", "dp", None),
        P(None, "dp", None),
        P(None, "tensor", "dp", None),
        P("dp", "tensor"),
        P("dp", "tensor"),
        P("dp", "tensor"),
        P("tensor", "dp"),
        P("dp", "tensor"),
        P("dp", "tensor"),
        P("tensor", "dp"),
        P("dp"),
        P("dp"),
    )
    return jax.shard_map(
        body,
        mesh=mesh,
        in_specs=placed,
        out_specs=(
            P(None, "tensor", "dp", None),
            P(None, "tensor", "dp", None),
            P("dp", "tensor"),
            P("dp", "tensor"),
            P("dp", "tensor"),
            P("tensor", "dp"),
            P("dp", "tensor"),
            P("dp", "tensor"),
            P("tensor", "dp"),
            P("dp"),
            P("dp"),
        ),
        check_vma=False,
    )
```

profile of v0, /device:TPU:0, one launch (start us, length us, event | category | flops | bytes accessed | tf_op | source)
XLA Modules:
  0.0 1807.1 jit_solution(9361418432597389148)
XLA Ops:
  62.5 25.8 %all-gather.24.cloned.1.call-done = bf16[1536,384]{1,0:T(8,128)(2,1)} async-done(((bf16[192,384]{1,0:T(8,128)(2,1)}), bf16[1536,384]{1,0:T(8,128)(2,1)}) %all-gather.24.cloned.1.call-update) | async-done | bytes 1179664 | tf_op jit(solution)/shard_map/all_gather | solution.py:259
  88.3 65.5 %all-gather.18.cloned.1.call-done = bf16[512,2,1536]{2,0,1:T(8,128)(2,1)} async-done(((bf16[128,2,1536]{2,0,1:T(8,128)(2,1)}), bf16[512,2,1536]{2,0,1:T(8,128)(2,1)}) %all-gather.18.cloned.1.call-update) | async-done | bytes 3145744 | tf_op jit(solution)/shard_map/all_gather | solution.py:97
  190.9 108.0 %reduce-scatter.16.cloned.1.call-done = f32[128,2,1536]{2,0,1:T(8,128)} async-done(((f32[512,2,1536]{2,0,1:T(8,128)}), f32[128,2,1536]{2,0,1:T(8,128)}) %reduce-scatter.16.cloned.1.call-update) | async-done | bytes 1572880 | tf_op jit(solution)/shard_map/reduce_scatter | solution.py:117
  307.0 26.5 %all-gather.30.cloned.1.call-done = bf16[1536,1024]{1,0:T(8,128)(2,1)} async-done(((bf16[192,1024]{1,0:T(8,128)(2,1)}), bf16[1536,1024]{1,0:T(8,128)(2,1)}) %all-gather.30.cloned.1.call-update) | async-done | bytes 3145744 | tf_op jit(solution)/shard_map/all_gather | solution.py:261
  333.6 34.1 %all-gather.32.cloned.1.call-done = bf16[1536,1024]{1,0:T(8,128)(2,1)} async-done(((bf16[192,1024]{1,0:T(8,128)(2,1)}), bf16[1536,1024]{1,0:T(8,128)(2,1)}) %all-gather.32.cloned.1.call-update) | async-done | bytes 3145744 | tf_op jit(solution)/shard_map/all_gather | solution.py:262
  367.7 65.6 %all-gather.28.cloned.1.call-done = bf16[512,2,1536]{2,0,1:T(8,128)(2,1)} async-done(((bf16[128,2,1536]{2,0,1:T(8,128)(2,1)}), bf16[512,2,1536]{2,0,1:T(8,128)(2,1)}) %all-gather.28.cloned.1.call-update) | async-done | bytes 3145744 | tf_op jit(solution)/shard_map/all_gather | solution.py:127
  445.4 52.0 %all-gather.44.cloned.1.call-done = bf16[1,512,2,1536]{3,1,2,0:T(8,128)(2,1)} async-done(((bf16[1,128,2,1536]{3,1,2,0:T(8,128)(2,1)}), bf16[1,512,2,1536]{3,1,2,0:T(8,128)(2,1)}) %all-gather.44.cloned.1.call-update) | async-done | bytes 3145744 | tf_op jit(solution)/shard_map/all_gather | solution.py:145
  497.4 32.7 %all-gather.34.cloned.1.call-done = bf16[1024,1536]{0,1:T(8,128)(2,1)} async-done(((bf16[1024,192]{0,1:T(8,128)(2,1)}), bf16[1024,1536]{0,1:T(8,128)(2,1)}) %all-gather.34.cloned.1.call-update) | async-done | bytes 3145744 | tf_op jit(solution)/shard_map/all_gather | solution.py:263
  551.9 60.5 %reduce-scatter.24.cloned.1.call-done = bf16[128,2,1536]{2,0,1:T(8,128)(2,1)} async-done(((bf16[512,2,1536]{2,0,1:T(8,128)(2,1)}), bf16[128,2,1536]{2,0,1:T(8,128)(2,1)}) %reduce-scatter.24.cloned.1.call-update) | async-done | bytes 786448 | tf_op jit(solution)/shard_map/reduce_scatter | solution.py:157
  617.2 63.4 %all-gather.40.cloned.1.call-done = bf16[512,2,1536]{2,0,1:T(8,128)(2,1)} async-done(((bf16[128,2,1536]{2,0,1:T(8,128)(2,1)}), bf16[512,2,1536]{2,0,1:T(8,128)(2,1)}) %all-gather.40.cloned.1.call-update) | async-done | bytes 3145744 | tf_op jit(solution)/shard_map/all_gather | solution.py:170
  729.1 57.9 %reduce-scatter.26.cloned.1.call-done = bf16[128,2,1536]{2,0,1:T(8,128)(2,1)} async-done(((bf16[512,2,1536]{2,0,1:T(8,128)(2,1)}), bf16[128,2,1536]{2,0,1:T(8,128)(2,1)}) %reduce-scatter.26.cloned.1.call-update) | async-done | bytes 786448 | tf_op jit(solution)/shard_map/reduce_scatter | solution.py:211
  790.6 63.5 %all-gather.36.cloned.1.call-done = bf16[512,2,1536]{2,0,1:T(8,128)(2,1)} async-done(((bf16[128,2,1536]{2,0,1:T(8,128)(2,1)}), bf16[512,2,1536]{2,0,1:T(8,128)(2,1)}) %all-gather.36.cloned.1.call-update) | async-done | bytes 3145744 | tf_op jit(solution)/shard_map/all_gather | solution.py:97
  903.5 101.2 %reduce-scatter.20.cloned.1.call-done = f32[128,2,1536]{2,0,1:T(8,128)} async-done(((f32[512,2,1536]{2,0,1:T(8,128)}), f32[128,2,1536]{2,0,1:T(8,128)}) %reduce-scatter.20.cloned.1.call-update) | async-done | bytes 1572880 | tf_op jit(solution)/shard_map/reduce_scatter | solution.py:117
  1007.4 60.4 %reduce-scatter.18.cloned.1.call-done = bf16[128,2,1536]{2,0,1:T(8,128)(2,1)} async-done(((bf16[512,2,1536]{2,0,1:T(8,128)(2,1)}), bf16[128,2,1536]{2,0,1:T(8,128)(2,1)}) %reduce-scatter.18.cloned.1.call-update) | async-done | bytes 786448 | tf_op jit(solution)/shard_map/reduce_scatter | solution.py:136
  1073.9 62.4 %all-gather.38.cloned.1.call-done = bf16[512,2,1536]{2,0,1:T(8,128)(2,1)} async-done(((bf16[128,2,1536]{2,0,1:T(8,128)(2,1)}), bf16[512,2,1536]{2,0,1:T(8,128)(2,1)}) %all-gather.38.cloned.1.call-update) | async-done | bytes 3145744 | tf_op jit(solution)/shard_map/all_gather | solution.py:127
  1148.5 52.1 %all-gather.46.cloned.1.call-done = bf16[1,512,2,1536]{3,1,2,0:T(8,128)(2,1)} async-done(((bf16[1,128,2,1536]{3,1,2,0:T(8,128)(2,1)}), bf16[1,512,2,1536]{3,1,2,0:T(8,128)(2,1)}) %all-gather.46.cloned.1.call-update) | async-done | bytes 3145744 | tf_op jit(solution)/shard_map/all_gather | solution.py:145
  1220.3 59.2 %reduce-scatter.28.cloned.1.call-done = bf16[128,2,1536]{2,0,1:T(8,128)(2,1)} async-done(((bf16[512,2,1536]{2,0,1:T(8,128)(2,1)}), bf16[128,2,1536]{2,0,1:T(8,128)(2,1)}) %reduce-scatter.28.cloned.1.call-update) | async-done | bytes 786448 | tf_op jit(solution)/shard_map/reduce_scatter | solution.py:157
  1447.3 47.4 %reduce-scatter.44.cloned.1.call-done = bf16[1024,192]{0,1:T(8,128)(2,1)} async-done(((bf16[1024,1536]{0,1:T(8,128)(2,1)}), bf16[1024,192]{0,1:T(8,128)(2,1)}) %reduce-scatter.44.cloned.1.call-update) | async-done | bytes 393232 | tf_op jit(solution)/shard_map/reduce_scatter | solution.py:292
  1496.6 38.0 %reduce-scatter.38.cloned.1.call-done = bf16[384,192]{0,1:T(8,128)(2,1)} async-done(((bf16[384,1536]{0,1:T(8,128)(2,1)}), bf16[384,192]{0,1:T(8,128)(2,1)}) %reduce-scatter.38.cloned.1.call-update) | async-done | bytes 147472 | tf_op jit(solution)/shard_map/reduce_scatter | solution.py:283
  1536.3 38.2 %reduce-scatter.32.cloned.1.call-done = bf16[192,384]{1,0:T(8,128)(2,1)} async-done(((bf16[1536,384]{1,0:T(8,128)(2,1)}), bf16[192,384]{1,0:T(8,128)(2,1)}) %reduce-scatter.32.cloned.1.call-update) | async-done | bytes 147472 | tf_op jit(solution)/shard_map/reduce_scatter | solution.py:274
  1576.0 38.7 %reduce-scatter.34.cloned.1.call-done = bf16[192,384]{1,0:T(8,128)(2,1)} async-done(((bf16[1536,384]{1,0:T(8,128)(2,1)}), bf16[192,384]{1,0:T(8,128)(2,1)}) %reduce-scatter.34.cloned.1.call-update) | async-done | bytes 147472 | tf_op jit(solution)/shard_map/reduce_scatter | solution.py:277
  1616.4 38.9 %reduce-scatter.36.cloned.1.call-done = bf16[192,384]{1,0:T(8,128)(2,1)} async-done(((bf16[1536,384]{1,0:T(8,128)(2,1)}), bf16[192,384]{1,0:T(8,128)(2,1)}) %reduce-scatter.36.cloned.1.call-update) | async-done | bytes 147472 | tf_op jit(solution)/shard_map/reduce_scatter | solution.py:280
  1656.9 61.1 %reduce-scatter.30.cloned.1.call-done = bf16[128,2,1536]{2,0,1:T(8,128)(2,1)} async-done(((bf16[512,2,1536]{2,0,1:T(8,128)(2,1)}), bf16[128,2,1536]{2,0,1:T(8,128)(2,1)}) %reduce-scatter.30.cloned.1.call-update) | async-done | bytes 786448 | tf_op jit(solution)/shard_map/reduce_scatter | solution.py:211
  1733.4 47.1 %reduce-scatter.22.cloned.1.call-done = bf16[128,2,1536]{2,0,1:T(8,128)(2,1)} async-done(((bf16[512,2,1536]{2,0,1:T(8,128)(2,1)}), bf16[128,2,1536]{2,0,1:T(8,128)(2,1)}) %reduce-scatter.22.cloned.1.call-update) | async-done | bytes 786448 | tf_op jit(solution)/shard_map/reduce_scatter | solution.py:136
  (399 shorter events, 489.7 us)
Async XLA Ops:
  9.4 144.4 %all-gather.18.cloned.1.call-start = ((), (), s32[]{:S(2)}) async-start(), calls=%async_computation.15 | async-start | bytes 3932160 | tf_op jit(solution)/shard_map/all_gather | solution.py:97
  35.3 148.1 %all-gather.26.cloned.1.call-start = ((), (), s32[]{:S(2)}) async-start(), calls=%async_computation.19 | async-start | bytes 1327104 | tf_op jit(solution)/shard_map/all_gather | solution.py:260
  35.9 263.1 %reduce-scatter.16.cloned.1.call-start = ((), (), s32[]{:S(2)}) async-start(), calls=%async_computation.20 | async-start | bytes 7864320 | tf_op jit(solution)/shard_map/reduce_scatter | solution.py:117
  189.3 144.2 %all-gather.30.cloned.1.call-start = ((), (), s32[]{:S(2)}) async-start(), calls=%async_computation.22 | async-start | bytes 3538944 | tf_op jit(solution)/shard_map/all_gather | solution.py:261
  190.1 177.6 %all-gather.32.cloned.1.call-start = ((), (), s32[]{:S(2)}) async-start(), calls=%async_computation.23 | async-start | bytes 3538944 | tf_op jit(solution)/shard_map/all_gather | solution.py:262
  190.8 242.4 %all-gather.28.cloned.1.call-start = ((), (), s32[]{:S(2)}) async-start(), calls=%async_computation.21 | async-start | bytes 3932160 | tf_op jit(solution)/shard_map/all_gather | solution.py:127
  301.7 195.6 %all-gather.44.cloned.1.call-start = ((), (), s32[]{:S(2)}) async-start(), calls=%async_computation.43 | async-start | bytes 3932160 | tf_op jit(solution)/shard_map/all_gather | solution.py:145
  306.2 223.9 %all-gather.34.cloned.1.call-start = ((), (), s32[]{:S(2)}) async-start(), calls=%async_computation.24 | async-start | bytes 3538944 | tf_op jit(solution)/shard_map/all_gather | solution.py:263
  307.0 305.4 %reduce-scatter.24.cloned.1.call-start = ((), (), s32[]{:S(2)}) async-start(), calls=%async_computation.30 | async-start | bytes 3932160 | tf_op jit(solution)/shard_map/reduce_scatter | solution.py:157
  551.9 128.8 %all-gather.40.cloned.1.call-start = ((), (), s32[]{:S(2)}) async-start(), calls=%async_computation.31 | async-start | bytes 3932160 | tf_op jit(solution)/shard_map/all_gather | solution.py:170
  617.2 169.8 %reduce-scatter.26.cloned.1.call-start = ((), (), s32[]{:S(2)}) async-start(), calls=%async_computation.32 | async-start | bytes 3932160 | tf_op jit(solution)/shard_map/reduce_scatter | solution.py:211
  790.6 214.1 %reduce-scatter.20.cloned.1.call-start = ((), (), s32[]{:S(2)}) async-start(), calls=%async_computation.27 | async-start | bytes 7864320 | tf_op jit(solution)/shard_map/reduce_scatter | solution.py:117
  895.1 172.7 %reduce-scatter.18.cloned.1.call-start = ((), (), s32[]{:S(2)}) async-start(), calls=%async_computation.25 | async-start | bytes 3932160 | tf_op jit(solution)/shard_map/reduce_scatter | solution.py:136
  902.9 233.4 %all-gather.38.cloned.1.call-start = ((), (), s32[]{:S(2)}) async-start(), calls=%async_computation.28 | async-start | bytes 3932160 | tf_op jit(solution)/shard_map/all_gather | solution.py:127
  1073.9 205.6 %reduce-scatter.28.cloned.1.call-start = ((), (), s32[]{:S(2)}) async-start(), calls=%async_computation.33 | async-start | bytes 3932160 | tf_op jit(solution)/shard_map/reduce_scatter | solution.py:157
  1284.2 146.2 %reduce-scatter.40.cloned.1.call-start = ((), (), s32[]{:S(2)}) async-start(), calls=%async_computation.40 | async-start | bytes 3538944 | tf_op jit(solution)/shard_map/reduce_scatter | solution.py:286
  1311.5 133.8 %reduce-scatter.42.cloned.1.call-start = ((), (), s32[]{:S(2)}) async-start(), calls=%async_computation.41 | async-start | bytes 3538944 | tf_op jit(solution)/shard_map/reduce_scatter | solution.py:289
  1312.2 182.4 %reduce-scatter.44.cloned.1.call-start = ((), (), s32[]{:S(2)}) async-start(), calls=%async_computation.42 | async-start | bytes 3538944 | tf_op jit(solution)/shard_map/reduce_scatter | solution.py:292
  1330.4 204.2 %reduce-scatter.38.cloned.1.call-start = ((), (), s32[]{:S(2)}) async-start(), calls=%async_computation.39 | async-start | bytes 1327104 | tf_op jit(solution)/shard_map/reduce_scatter | solution.py:283
  1392.3 182.1 %reduce-scatter.32.cloned.1.call-start = ((), (), s32[]{:S(2)}) async-start(), calls=%async_computation.36 | async-start | bytes 1327104 | tf_op jit(solution)/shard_map/reduce_scatter | solution.py:274
  1411.9 202.9 %reduce-scatter.34.cloned.1.call-start = ((), (), s32[]{:S(2)}) async-start(), calls=%async_computation.37 | async-start | bytes 1327104 | tf_op jit(solution)/shard_map/reduce_scatter | solution.py:277
  1412.5 242.8 %reduce-scatter.36.cloned.1.call-start = ((), (), s32[]{:S(2)}) async-start(), calls=%async_computation.38 | async-start | bytes 1327104 | tf_op jit(solution)/shard_map/reduce_scatter | solution.py:280
  1413.2 304.8 %reduce-scatter.30.cloned.1.call-start = ((), (), s32[]{:S(2)}) async-start(), calls=%async_computation.35 | async-start | bytes 3932160 | tf_op jit(solution)/shard_map/reduce_scatter | solution.py:211
  1421.7 358.8 %reduce-scatter.22.cloned.1.call-start = ((), (), s32[]{:S(2)}) async-start(), calls=%async_computation.29 | async-start | bytes 3932160 | tf_op jit(solution)/shard_map/reduce_scatter | solution.py:136
  (105 other events, 5185.5 us)
Sparse Core Ops, SparseCore 0:
  90.3 63.4 all-gather.17
  189.5 109.4 reduce-scatter.15
  300.8 32.6 all-gather.29
  369.8 63.4 all-gather.27
  435.3 62.0 all-gather.43
  552.0 60.3 reduce-scatter.23
  617.3 63.3 all-gather.39
  727.9 59.0 reduce-scatter.25
  790.7 63.3 all-gather.35
  895.2 109.4 reduce-scatter.19
  1006.8 60.8 reduce-scatter.17
  1073.0 63.3 all-gather.37
  1138.5 62.0 all-gather.45
  1220.4 59.0 reduce-scatter.27
  1284.3 63.3 all-gather.41
  1351.1 44.6 reduce-scatter.39
  1399.2 46.0 reduce-scatter.41
  1448.6 46.0 reduce-scatter.43
  1497.9 36.6 reduce-scatter.37
  1537.7 36.6 reduce-scatter.31
  1578.1 36.6 reduce-scatter.33
  1618.6 36.6 reduce-scatter.35
  1657.6 60.3 reduce-scatter.29
  1720.2 60.2 reduce-scatter.21
  (6 shorter events, 159.8 us)
where the time goes:
time: 1810 us
  waiting for transfers between devices  1360 us (75%)
  matrix products  237 us (13%)
  other arithmetic  91.4 us (5%)
  local copies, waits for them, and re-layouts  60 us (3%)
  blocking collectives  40.5 us (2%)
    reduce_scatter x2, waiting for transfers between devices, micro_step(): lax.psum_scatter(jnp.einsum('tgc,cd->tgd', rows_here, w_out, preferred_el...  209 us
    all_gather x2, waiting for transfers between devices, micro_step(): normed_all = lax.all_gather(normed_one, 'tensor', axis=0, tiled=True)  129 us
    all_gather x2, waiting for transfers between devices, micro_step(): normed_more = lax.all_gather(normed_two, 'tensor', axis=0, tiled=True)  128 us
    reduce_scatter x2, waiting for transfers between devices, micro_step(): lax.psum_scatter(jnp.einsum('tgf,df->tgd', rows_here, w_gate_up, preferre...  120 us
    reduce_scatter x2, waiting for transfers between devices, micro_step(): lax.psum_scatter(jnp.einsum('tgc,dc->tgd', rows_here, w_joint, preferred_...  119 us
    reduce_scatter x2, waiting for transfers between devices, micro_step(): lax.psum_scatter(jnp.einsum('tgf,fd->tgd', rows_here, w_down, preferred_e...  107 us
    all_gather x2, waiting for transfers between devices, micro_step(): upstream_all = lax.all_gather(upstream, 'tensor', axis=0, tiled=True)  104 us
    all_gather x2, waiting for transfers between devices, micro_step(): attn_grad_all = lax.all_gather(attn_grad, 'tensor', axis=0, tiled=True)  80.2 us
  transfers between devices with their start and end apart: 30, of which 27 were waited for; matrix products, arithmetic and copies ran while one was open for 12% of the time, Pallas kernels for 0%

commit v1 on v0

--- a/solution.py
+++ b/solution.py
@@ -234,7 +234,7 @@
     return (output, input_grad, param_grads)
 
 
-def body(
+def sharded_body(
     block_input,
     lengths,
     out_grad,
@@ -315,6 +315,214 @@
     )
 
 
+def gather_full(shard):
+    rows, cols = shard.shape
+    dp_size = lax.axis_size("dp")
+    z_size = lax.axis_size("tensor")
+    full = lax.all_gather(shard, ("dp", "tensor"), axis=0, tiled=True)
+    return full.reshape(dp_size, z_size, rows, cols).transpose(0, 2, 1, 3).reshape(
+        dp_size * rows, z_size * cols
+    )
+
+
+def scatter_full(grad):
+    dp_size = lax.axis_size("dp")
+    z_size = lax.axis_size("tensor")
+    rows = grad.shape[0] // dp_size
+    cols = grad.shape[1] // z_size
+    flat = (
+        grad.reshape(dp_size, rows, z_size, cols)
+        .transpose(0, 2, 1, 3)
+        .reshape(dp_size * z_size * rows, cols)
+    )
+    return lax.psum_scatter(
+        flat, ("dp", "tensor"), scatter_dimension=0, tiled=True
+    ).astype(jnp.float32)
+
+
+def to_group(values):
+    micro, rows, groups, width = values.shape
+    parts = values.transpose(0, 2, 1, 3).reshape(micro * groups, rows, width)
+    moved = lax.all_to_all(parts, "tensor", 0, 0, tiled=True)
+    return moved.reshape(micro * groups * rows, width)
+
+
+def from_group(values, micro, groups):
+    rows = values.shape[0] // (micro * groups)
+    width = values.shape[1]
+    parts = values.reshape(micro * groups, rows, width)
+    moved = lax.all_to_all(parts, "tensor", 0, 0, tiled=True)
+    return moved.reshape(micro, groups, rows, width).transpose(0, 2, 1, 3)
+
+
+def dot_tt(left, right, dims):
+    return lax.dot_general(left, right, (dims, ((), ())), preferred_element_type=jnp.float32)
+
+
+def turn(values, cos_table, sin_table, sign):
+    half = HD // 2
+    first_half = values[..., :half]
+    second_half = values[..., half:]
+    return jnp.concatenate(
+        [
+            first_half * cos_table - sign * second_half * sin_table,
+            second_half * cos_table + sign * first_half * sin_table,
+        ],
+        axis=-1,
+    )
+
+
+def group_body(
+    block_input,
+    lengths,
+    out_grad,
+    w_query,
+    w_key,
+    w_value,
+    w_out,
+    w_gate,
+    w_up,
+    w_down,
+    attn_gain,
+    ffn_gain,
+):
+    micro, _, groups, width = block_input.shape
+    head_cols = w_query.shape[1] * lax.axis_size("tensor")
+    heads = head_cols // HD
+    bf16 = jnp.bfloat16
+    f32 = jnp.float32
+    tokens_in = to_group(block_input)
+    upstream = to_group(out_grad)
+    own_lengths = lax.dynamic_slice_in_dim(
+        lengths.reshape(micro * groups, 3), lax.axis_index("tensor"), 1, 0
+    )
+    gains = lax.all_gather(jnp.stack([attn_gain, ffn_gain]), "dp", axis=1, tiled=True)
+    gain_one = gains[0].astype(f32)
+    gain_two = gains[1].astype(f32)
+    wq = gather_full(w_query)
+    wk = gather_full(w_key)
+    wv = gather_full(w_value)
+    wo = gather_full(w_out.T)
+    wg = gather_full(w_gate)
+    wu = gather_full(w_up)
+    wd = gather_full(w_down.T)
+
+    segment, cos_table, sin_table = layout_tables(own_lengths)
+    seg = segment[:, 0]
+    cos_table = cos_table[:, 0, None, :]
+    sin_table = sin_table[:, 0, None, :]
+    index = jnp.arange(GTOK, dtype=jnp.int32)
+    allowed = (index[None, :] <= index[:, None]) & (
+        (seg[None, :] == 0) | (seg[None, :] == seg[:, None])
+    )
+    residual = tokens_in.astype(f32)
+    scale_one = rms_scale(residual)
+    unit_one = residual * scale_one
+    normed_one = (unit_one * gain_one).astype(bf16)
+    contract = ((1,), (0,))
+    contract_t = ((1,), (1,))
+    contract_tok = ((0,), (0,))
+    split = (GTOK, heads, HD)
+    queries = turn(
+        dot_tt(normed_one, wq, contract).reshape(split), cos_table, sin_table, 1.0
+    ).astype(bf16)
+    keys = turn(
+        dot_tt(normed_one, wk, contract).reshape(split), cos_table, sin_table, 1.0
+    ).astype(bf16)
+    values = dot_tt(normed_one, wv, contract).reshape(split).astype(bf16)
+    scale = HD ** (-0.5)
+
+    def score(qs, ks):
+        raw = jnp.einsum("the,she->hts", qs, ks, preferred_element_type=f32) * scale
+        return jnp.where(allowed[None], raw, MASKED)
+
+    scores = score(queries, keys)
+    row_max = jnp.max(scores, axis=-1, keepdims=True)
+    log_total = row_max + jnp.log(jnp.sum(jnp.exp(scores - row_max), axis=-1, keepdims=True))
+    probs = jnp.exp(scores - log_total).astype(bf16)
+    mix = (
+        jnp.einsum("hts,she->the", probs, values, preferred_element_type=f32)
+        .astype(bf16)
+        .reshape(GTOK, head_cols)
+    )
+    middle = residual + dot_tt(mix, wo, contract_t)
+    scale_two = rms_scale(middle)
+    unit_two = middle * scale_two
+    normed_two = (unit_two * gain_two).astype(bf16)
+    gate_vals = dot_tt(normed_two, wg, contract)
+    up_vals = dot_tt(normed_two, wu, contract)
+    sigmoid_gate = jax.nn.sigmoid(gate_vals)
+    silu_gate = gate_vals * sigmoid_gate
+    hidden = (silu_gate * up_vals).astype(bf16)
+    output = (middle + dot_tt(hidden, wd, contract_t)).astype(bf16)
+    out_final = from_group(output, micro, groups)
+
+    grad_down = dot_tt(upstream, hidden, contract_tok).astype(bf16)
+    share_down = scatter_full(grad_down).T
+    hidden_grad = dot_tt(upstream, wd, contract)
+    up_grad = (hidden_grad * silu_gate).astype(bf16)
+    gate_grad = (
+        hidden_grad * up_vals * (sigmoid_gate * (1.0 + gate_vals * (1.0 - sigmoid_gate)))
+    ).astype(bf16)
+    share_gate = scatter_full(dot_tt(normed_two, gate_grad, contract_tok).astype(bf16))
+    share_up = scatter_full(dot_tt(normed_two, up_grad, contract_tok).astype(bf16))
+    normed_two_grad = dot_tt(gate_grad, wg, contract_t) + dot_tt(up_grad, wu, contract_t)
+    gain_two_grad = jnp.sum(normed_two_grad * unit_two, axis=0)
+    middle_grad = upstream.astype(f32) + norm_back(
+        normed_two_grad, unit_two, gain_two, scale_two
+    )
+    attn_grad = middle_grad.astype(bf16)
+    share_out = scatter_full(dot_tt(attn_grad, mix, contract_tok).astype(bf16)).T
+    mix_grad = dot_tt(attn_grad, wo, contract).astype(bf16).reshape(split)
+    probs_full = jnp.exp(score(queries, keys) - log_total)
+    prob_grad = jnp.einsum("the,she->hts", mix_grad, values, preferred_element_type=f32)
+    value_grad = jnp.einsum(
+        "hts,the->she", probs_full.astype(bf16), mix_grad, preferred_element_type=f32
+    )
+    centre = jnp.sum(probs_full * prob_grad, axis=-1, keepdims=True)
+    score_grad = (probs_full * (prob_grad - centre)).astype(bf16)
+    query_grad = jnp.einsum("hts,she->the", score_grad, keys, preferred_element_type=f32) * scale
+    key_grad = jnp.einsum("hts,the->she", score_grad, queries, preferred_element_type=f32) * scale
+    flat = (GTOK, head_cols)
+    dq = turn(query_grad, cos_table, sin_table, -1.0).reshape(flat).astype(bf16)
+    dk = turn(key_grad, cos_table, sin_table, -1.0).reshape(flat).astype(bf16)
+    dv = value_grad.reshape(flat).astype(bf16)
+    normed_one_grad = (
+        dot_tt(dq, wq, contract_t) + dot_tt(dk, wk, contract_t) + dot_tt(dv, wv, contract_t)
+    )
+    gain_one_grad = jnp.sum(normed_one_grad * unit_one, axis=0)
+    input_grad = (
+        middle_grad + norm_back(normed_one_grad, unit_one, gain_one, scale_one)
+    ).astype(bf16)
+    in_grad_final = from_group(input_grad, micro, groups)
+    share_query = scatter_full(dot_tt(normed_one, dq, contract_tok).astype(bf16))
+    share_key = scatter_full(dot_tt(normed_one, dk, contract_tok).astype(bf16))
+    share_value = scatter_full(dot_tt(normed_one, dv, contract_tok).astype(bf16))
+    gain_sums = lax.psum(jnp.stack([gain_one_grad, gain_two_grad]), ("dp", "tensor"))
+    gain_rows = attn_gain.shape[0]
+    own_gains = lax.dynamic_slice_in_dim(gain_sums, lax.axis_index("dp") * gain_rows, gain_rows, 1)
+    return (
+        out_final,
+        in_grad_final,
+        share_query,
+        share_key,
+        share_value,
+        share_out,
+        share_gate,
+        share_up,
+        share_down,
+        own_gains[0],
+        own_gains[1],
+    )
+
+
+def body(*operands):
+    micro, _, groups, _ = operands[0].shape
+    if micro * groups == lax.axis_size("tensor"):
+        return group_body(*operands)
+    return sharded_body(*operands)
+
+
 def solution(mesh):
     placed = (
         P(None, "tensor", "dp", None),

time: 1810 us -> 1670 us (0.923)
  waiting for transfers between devices: 1360 us -> 945 us
  local copies, waits for them, and re-layouts: 60 us -> 339 us
  other arithmetic: 91.4 us -> 57.3 us
  blocking collectives: 40.5 us -> 65.9 us
    reduce_scatter x15 -> x7, waiting for transfers between devices: 769 us -> 514 us  [scatter_full(): lax.psum_scatter(flat, ('dp', 'tensor'), scatter_dimension=0, tiled=True)]
    all_gather x15 -> x7, waiting for transfers between devices: 582 us -> 368 us  [gather_full(): full = lax.all_gather(shard, ('dp', 'tensor'), axis=0, tiled=True)]
    reshape x6 -> x14, local copies, waits for them, and re-layouts: 7.65 us -> 174 us  [the longest x7 101 us: scatter_full(): grad.reshape(dp_size, rows, z_size, cols).transpose(0, 2, 1, 3)]
    transpose x0 -> x7, local copies, waits for them, and re-layouts: none -> 61.5 us  [scatter_full(): flat = grad.reshape(dp_size, rows, z_size, cols).transpose(0, 2, 1, 3).re...]
    all_to_all x0 -> x4, waiting for transfers between devices: none -> 59.8 us  [the longest x2 33.8 us: from_group(): moved = lax.all_to_all(parts, 'tensor', 0, 0, tiled=True)]
    psum x1, blocking collectives: 10.9 us -> 56.9 us  [group_body(): lax.psum(jnp.stack([gain_one_grad, gain_two_grad]), ('dp', 'tensor'))]
    unnamed x207 -> x144, local copies, waits for them, and re-layouts: 26.6 us -> 62.7 us
    unnamed x2 -> x0, blocking collectives: 29.6 us -> none
  transfers between devices with their start and end apart: 30 -> 18, of which waited for: 27 -> 13; matrix products, arithmetic and copies ran while one was open for 12% -> 31% of each run, Pallas kernels for 0% -> 0%
where the time goes in v1:
time: 1670 us; the launch traced here: 1660 us
  waiting for transfers between devices  945 us (57%)
  local copies, waits for them, and re-layouts  339 us (20%)
  matrix products  219 us (13%)
  blocking collectives  65.9 us (4%)
  other arithmetic  57.3 us (3%)
  starting transfers between devices  18.7 us (1%)
    reduce_scatter x7, waiting for transfers between devices, scatter_full(): lax.psum_scatter(flat, ('dp', 'tensor'), scatter_dimension=0, tiled=True)  514 us
    all_gather x7, waiting for transfers between devices, gather_full(): full = lax.all_gather(shard, ('dp', 'tensor'), axis=0, tiled=True)  368 us
    dot_general x21, matrix products, dot_tt(): lax.dot_general(left, right, (dims, ((), ())), preferred_element_type=jnp...  155 us
    reshape x7, local copies, waits for them, and re-layouts, scatter_full(): grad.reshape(dp_size, rows, z_size, cols).transpose(0, 2, 1, 3)  101 us
    reshape x7, local copies, waits for them, and re-layouts, gather_full(): full.reshape(dp_size, z_size, rows, cols).transpose(0, 2, 1, 3)  72.7 us
    unnamed x144, local copies, waits for them, and re-layouts  62.7 us
    transpose x7, local copies, waits for them, and re-layouts, scatter_full(): flat = grad.reshape(dp_size, rows, z_size, cols).transpose(0, 2, 1, 3).re...  61.5 us
    psum x1, blocking collectives, group_body(): lax.psum(jnp.stack([gain_one_grad, gain_two_grad]), ('dp', 'tensor'))  56.9 us
  transfers between devices with their start and end apart: 18, of which 13 were waited for; matrix products, arithmetic and copies ran while one was open for 31% of the time, Pallas kernels for 0%

profile of v1, /device:TPU:0, one launch (start us, length us, event | category | flops | bytes accessed | tf_op | source)
XLA Modules:
  0.0 1661.5 jit_solution(5085890962014931335)
XLA Ops:
  37.2 26.0 %all-to-all-done = bf16[4,128,1536]{2,1,0:T(8,128)(2,1)S(1)} async-done(((bf16[4,128,1536]{2,1,0:T(8,128)(2,1)}), bf16[4,128,1536]{2,1,0:T(8,128)(2,1)S(1)}, u32[]{:S(2)}, u32[]{:S(2)}) %all-to-all-start) | async-done | bytes 1572896 | tf_op jit(solution)/shard_map/all_to_all | solution.py:346
  69.4 43.3 %all-gather.11.cloned.1.call-done = bf16[6144,384]{1,0:T(8,128)(2,1)} async-done(((bf16[192,384]{1,0:T(8,128)(2,1)}), bf16[6144,384]{1,0:T(8,128)(2,1)}) %all-gather.11.cloned.1.call-update) | async-done | bytes 4718608 | tf_op jit(solution)/shard_map/all_gather | solution.py:322
  128.5 53.1 %all-gather.13.cloned.1.call-done = bf16[6144,384]{1,0:T(8,128)(2,1)} async-done(((bf16[192,384]{1,0:T(8,128)(2,1)}), bf16[6144,384]{1,0:T(8,128)(2,1)}) %all-gather.13.cloned.1.call-update) | async-done | bytes 4718608 | tf_op jit(solution)/shard_map/all_gather | solution.py:322
  197.1 49.2 %all-gather.9.cloned.1.call-done = bf16[6144,384]{1,0:T(8,128)(2,1)} async-done(((bf16[192,384]{1,0:T(8,128)(2,1)}), bf16[6144,384]{1,0:T(8,128)(2,1)}) %all-gather.9.cloned.1.call-update) | async-done | bytes 4718608 | tf_op jit(solution)/shard_map/all_gather | solution.py:322
  262.1 48.8 %all-gather.15.cloned.1.call-done = bf16[6144,384]{1,0:T(8,128)(2,1)} async-done(((bf16[192,384]{1,0:T(8,128)(2,1)}), bf16[6144,384]{1,0:T(8,128)(2,1)}) %all-gather.15.cloned.1.call-update) | async-done | bytes 4718608 | tf_op jit(solution)/shard_map/all_gather | solution.py:322
  368.3 38.9 %all-gather.17.cloned.1.call-done = bf16[6144,1024]{1,0:T(8,128)(2,1)} async-done(((bf16[192,1024]{1,0:T(8,128)(2,1)}), bf16[6144,1024]{1,0:T(8,128)(2,1)}) %all-gather.17.cloned.1.call-update) | async-done | bytes 12582928 | tf_op jit(solution)/shard_map/all_gather | solution.py:322
  407.2 16.2 copy.103
  441.6 62.1 %all-gather.19.cloned.1.call-done = bf16[6144,1024]{1,0:T(8,128)(2,1)} async-done(((bf16[192,1024]{1,0:T(8,128)(2,1)}), bf16[6144,1024]{1,0:T(8,128)(2,1)}) %all-gather.19.cloned.1.call-update) | async-done | bytes 12582928 | tf_op jit(solution)/shard_map/all_gather | solution.py:322
  503.8 16.2 copy.104
  528.0 72.4 %all-gather.21.cloned.1.call-done = bf16[6144,1024]{1,0:T(8,128)(2,1)} async-done(((bf16[192,1024]{1,0:T(8,128)(2,1)}), bf16[6144,1024]{1,0:T(8,128)(2,1)}) %all-gather.21.cloned.1.call-update) | async-done | bytes 12582928 | tf_op jit(solution)/shard_map/all_gather | solution.py:322
  600.5 16.3 copy.105
  633.9 19.3 %multiply_convert_fusion.1 = (bf16[512,4096]{1,0:T(8,128)(2,1)}, bf16[512,4096]{1,0:T(8,128)(2,1)S(1)}, bf16[512,4096]{1,0:T(8,128)(2,1)}) fusion(f32[512,4096]{1,0:T(8,128)} %fusion.25, f32[512,4096]{1,0:T(8,128)} %fusion.26, bf16[512,1536]{1,0:T(8,128)(2,1)S(1)} %bitcast.216, bf16[1536,4096]{1,0:T(8,128)(2,1)} %bitcast.201), kind=kOutput, calls=%fused_computation.11 | convolution fusion | flops 6473908224 | bytes 43515904 | tf_op jit(solution)/shard_map/dot_general | solution.py:359
  717.7 17.9 %multiply_reduce_fusion = (f32[24,512]{1,0:T(8,128)S(1)}, f32[24,512,512]{1,2,0:T(8,128)}) fusion(f32[24,512,512]{1,2,0:T(8,128)} %get-tuple-element.75, f32[24,512]{1,0:T(8,128)S(1)} %copy-done.38, pred[512,512]{0,1:T(8,128)(4,1)S(1)} %copy-done.16, bf16[512,24,64]{0,2,1:T(8,128)(2,1)} %bitcast.213, bf16[512,24,64]{0,2,1:T(8,128)(2,1)} %copy-done.23), kind=kOutput, calls=%fused_computation.1 | convolution fusion | flops 836751360 | bytes 53837824 | tf_op jit(solution)/shard_map/the,she->hts/dot_general | solution.py:478
  735.5 18.5 %multiply_convert_fusion = bf16[24,512,512]{1,2,0:T(8,128)(2,1)S(1)} fusion(f32[24,512,512]{1,2,0:T(8,128)} %get-tuple-element.80, f32[24,512,512]{1,2,0:T(8,128)} %get-tuple-element.75, f32[24,512]{1,0:T(8,128)S(1)} %get-tuple-element.79, f32[24,512]{1,0:T(8,128)S(1)} %copy-done.38, pred[512,512]{0,1:T(8,128)(4,1)S(1)} %copy-done.16), kind=kLoop, calls=%fused_computation | loop fusion | flops 37748736 | bytes 63275008 | tf_op jit(solution)/shard_map/convert_element_type | solution.py:483
  849.1 21.4 %reshape.485 = bf16[8,192,4,1024]{3,2,1,0:T(4,128)(2,1)} reshape(bf16[1536,4096]{1,0:T(8,128)(2,1)} %convolution_convert_fusion.2) | data formatting | bytes 25165824 | tf_op jit(solution)/shard_map/reshape | solution.py:334
  895.9 21.3 %reshape.487 = bf16[8,192,4,1024]{3,2,1,0:T(4,128)(2,1)} reshape(bf16[1536,4096]{1,0:T(8,128)(2,1)} %convolution_convert_fusion.1) | data formatting | bytes 25165824 | tf_op jit(solution)/shard_map/reshape | solution.py:334
  943.7 16.9 %copy.117 = bf16[1536,4096]{1,0:T(8,128)(2,1)} copy(bf16[1536,4096]{0,1:T(8,128)(2,1)} %fusion.2) | data formatting | bytes 25165824 | tf_op jit(solution)/shard_map/convert_element_type | solution.py:460
  960.6 21.4 %reshape.489 = bf16[8,192,4,1024]{3,2,1,0:T(4,128)(2,1)} reshape(bf16[1536,4096]{1,0:T(8,128)(2,1)} %copy.117) | data formatting | bytes 25165824 | tf_op jit(solution)/shard_map/reshape | solution.py:334
  1026.8 33.8 %all-to-all-done.3 = bf16[4,128,1536]{2,1,0:T(8,128)(2,1)} async-done(((bf16[4,128,1536]{2,1,0:T(8,128)(2,1)}), bf16[4,128,1536]{2,1,0:T(8,128)(2,1)}, u32[]{:S(2)}, u32[]{:S(2)}) %all-to-all-start.3) | async-done | bytes 1572896 | tf_op jit(solution)/shard_map/all_to_all | solution.py:354
  1064.2 56.9 %psum.7 = f32[2,1536]{1,0:T(2,128)S(1)} all-reduce(f32[2,1536]{1,0:T(2,128)S(1)} %pad_maximum_fusion.8), channel_id=1, replica_groups=mesh['dp'=8,'tensor'=4] {'dp','tensor'}, use_global_device_ids=true, to_apply=%region_16.17 | all-reduce | flops 3072 | bytes 24576 | tf_op jit(solution)/shard_map/psum | solution.py:501
  1133.6 39.7 %reduce-scatter.14.cloned.1.call-done = bf16[192,384]{1,0:T(8,128)(2,1)} async-done(((bf16[6144,384]{1,0:T(8,128)(2,1)}), bf16[192,384]{1,0:T(8,128)(2,1)}) %reduce-scatter.14.cloned.1.call-update) | async-done | bytes 147472 | tf_op jit(solution)/shard_map/reduce_scatter | solution.py:338
  1175.0 158.2 %reduce-scatter.16.cloned.1.call-done = bf16[192,1024]{1,0:T(8,128)(2,1)} async-done(((bf16[6144,1024]{1,0:T(8,128)(2,1)}), bf16[192,1024]{1,0:T(8,128)(2,1)}) %reduce-scatter.16.cloned.1.call-update) | async-done | bytes 393232 | tf_op jit(solution)/shard_map/reduce_scatter | solution.py:338
  1335.2 157.9 %reduce-scatter.18.cloned.1.call-done = bf16[192,1024]{1,0:T(8,128)(2,1)} async-done(((bf16[6144,1024]{1,0:T(8,128)(2,1)}), bf16[192,1024]{1,0:T(8,128)(2,1)}) %reduce-scatter.18.cloned.1.call-update) | async-done | bytes 393232 | tf_op jit(solution)/shard_map/reduce_scatter | solution.py:338
  1495.1 157.7 %reduce-scatter.20.cloned.1.call-done = bf16[192,1024]{1,0:T(8,128)(2,1)} async-done(((bf16[6144,1024]{1,0:T(8,128)(2,1)}), bf16[192,1024]{1,0:T(8,128)(2,1)}) %reduce-scatter.20.cloned.1.call-update) | async-done | bytes 393232 | tf_op jit(solution)/shard_map/reduce_scatter | solution.py:338
  (271 shorter events, 461.7 us)
Async XLA Ops:
  7.2 105.5 %all-gather.11.cloned.1.call-start = ((), (), s32[]{:S(2)}) async-start(), calls=%async_computation.12 | async-start | bytes 4866048 | tf_op jit(solution)/shard_map/all_gather | solution.py:322
  7.9 173.6 %all-gather.13.cloned.1.call-start = ((), (), s32[]{:S(2)}) async-start(), calls=%async_computation.13 | async-start | bytes 4866048 | tf_op jit(solution)/shard_map/all_gather | solution.py:322
  8.7 237.6 %all-gather.9.cloned.1.call-start = ((), (), s32[]{:S(2)}) async-start(), calls=%async_computation.11 | async-start | bytes 4866048 | tf_op jit(solution)/shard_map/all_gather | solution.py:322
  9.4 301.5 %all-gather.15.cloned.1.call-start = ((), (), s32[]{:S(2)}) async-start(), calls=%async_computation.14 | async-start | bytes 4866048 | tf_op jit(solution)/shard_map/all_gather | solution.py:322
  10.0 397.2 %all-gather.17.cloned.1.call-start = ((), (), s32[]{:S(2)}) async-start(), calls=%async_computation.15 | async-start | bytes 12976128 | tf_op jit(solution)/shard_map/all_gather | solution.py:322
  10.6 493.2 %all-gather.19.cloned.1.call-start = ((), (), s32[]{:S(2)}) async-start(), calls=%async_computation.16 | async-start | bytes 12976128 | tf_op jit(solution)/shard_map/all_gather | solution.py:322
  11.2 589.3 %all-gather.21.cloned.1.call-start = ((), (), s32[]{:S(2)}) async-start(), calls=%async_computation.17 | async-start | bytes 12976128 | tf_op jit(solution)/shard_map/all_gather | solution.py:322
  14.8 48.5 %all-to-all-start = ((bf16[4,128,1536]{2,1,0:T(8,128)(2,1)}), bf16[4,128,1536]{2,1,0:T(8,128)(2,1)S(1)}, u32[]{:S(2)}, u32[]{:S(2)}) async-start(bf16[4,128,1536]{2,1,0:T(8,128)(2,1)} %bitcast.1), calls=%async_computation | async-start | bytes 3145728 | tf_op jit(solution)/shard_map/all_to_all | solution.py:346
  37.0 287.7 %copy-start.35 = (f32[512,32]{0,1:T(8,128)}, f32[512,32]{0,1:T(8,128)S(1)}, u32[]{:S(2)}) copy-start(f32[512,32]{0,1:T(8,128)S(1)} %get-tuple-element.69) | copy-start | bytes 196612
  37.2 313.7 %copy-start.15 = (pred[512,512]{0,1:T(8,128)(4,1)}, pred[512,512]{0,1:T(8,128)(4,1)S(1)}, u32[]{:S(2)}) copy-start(pred[512,512]{0,1:T(8,128)(4,1)S(1)} %fusion.5) | copy-start | bytes 786436
  63.3 299.9 %copy-start.3 = (bf16[4,128,1536]{2,1,0:T(8,128)(2,1)}, bf16[4,128,1536]{2,1,0:T(8,128)(2,1)S(1)}, u32[]{:S(2)}) copy-start(bf16[4,128,1536]{2,1,0:T(8,128)(2,1)S(1)} %all-to-all-done) | copy-start | bytes 4718596
  63.3 570.6 %all-to-all-start.2 = ((bf16[4,128,1536]{2,1,0:T(8,128)(2,1)}), bf16[4,128,1536]{2,1,0:T(8,128)(2,1)S(1)}, u32[]{:S(2)}, u32[]{:S(2)}) async-start(bf16[4,128,1536]{2,1,0:T(8,128)(2,1)} %bitcast.41), calls=%async_computation.2 | async-start | bytes 3145728 | tf_op jit(solution)/shard_map/all_to_all | solution.py:346
  66.8 1061.9 %reduce-scatter.12.cloned.1.call-start = ((), (), s32[]{:S(2)}) async-start(), calls=%async_computation.20 | async-start | bytes 4866048 | tf_op jit(solution)/shard_map/reduce_scatter | solution.py:338
  368.3 256.7 %copy-start.33 = (bf16[512,1536]{1,0:T(8,128)(2,1)}, bf16[512,1536]{1,0:T(8,128)(2,1)S(1)}, u32[]{:S(2)}) copy-start(bf16[512,1536]{1,0:T(8,128)(2,1)S(1)} %multiply_convert_fusion.4) | copy-start | bytes 4718596
  679.3 136.0 %copy-start.6 = (f32[512,1536]{1,0:T(8,128)}, f32[512,1536]{1,0:T(8,128)S(1)}, u32[]{:S(2)}) copy-start(f32[512,1536]{1,0:T(8,128)S(1)} %multiply_add_fusion) | copy-start | bytes 9437188
  717.6 412.7 %reduce-scatter.10.cloned.1.call-start = ((), (), s32[]{:S(2)}) async-start(), calls=%async_computation.19 | async-start | bytes 4866048 | tf_op jit(solution)/shard_map/reduce_scatter | solution.py:338
  793.5 338.4 %reduce-scatter.8.cloned.1.call-start = ((), (), s32[]{:S(2)}) async-start(), calls=%async_computation.18 | async-start | bytes 4866048 | tf_op jit(solution)/shard_map/reduce_scatter | solution.py:338
  815.3 358.1 %reduce-scatter.14.cloned.1.call-start = ((), (), s32[]{:S(2)}) async-start(), calls=%async_computation.21 | async-start | bytes 4866048 | tf_op jit(solution)/shard_map/reduce_scatter | solution.py:338
  835.8 497.4 %reduce-scatter.16.cloned.1.call-start = ((), (), s32[]{:S(2)}) async-start(), calls=%async_computation.22 | async-start | bytes 12976128 | tf_op jit(solution)/shard_map/reduce_scatter | solution.py:338
  883.7 609.4 %reduce-scatter.18.cloned.1.call-start = ((), (), s32[]{:S(2)}) async-start(), calls=%async_computation.23 | async-start | bytes 12976128 | tf_op jit(solution)/shard_map/reduce_scatter | solution.py:338
  930.4 722.3 %reduce-scatter.20.cloned.1.call-start = ((), (), s32[]{:S(2)}) async-start(), calls=%async_computation.24 | async-start | bytes 12976128 | tf_op jit(solution)/shard_map/reduce_scatter | solution.py:338
  1010.2 50.4 %all-to-all-start.3 = ((bf16[4,128,1536]{2,1,0:T(8,128)(2,1)}), bf16[4,128,1536]{2,1,0:T(8,128)(2,1)}, u32[]{:S(2)}, u32[]{:S(2)}) async-start(bf16[4,128,1536]{2,1,0:T(8,128)(2,1)} %bitcast.215), calls=%async_computation.3 | async-start | bytes 3145728 | tf_op jit(solution)/shard_map/all_to_all | solution.py:354
  1060.5 65.4 %all-to-all-start.1 = ((bf16[4,128,1536]{2,1,0:T(8,128)(2,1)}), bf16[4,128,1536]{2,1,0:T(8,128)(2,1)S(1)}, u32[]{:S(2)}, u32[]{:S(2)}) async-start(bf16[4,128,1536]{2,1,0:T(8,128)(2,1)} %bitcast.239), calls=%async_computation.1 | async-start | bytes 3145728 | tf_op jit(solution)/shard_map/all_to_all | solution.py:354
  1125.9 528.8 %copy-start.1 = (s32[2,2,3]{2,1,0:T(2,128)S(1)}, s32[2,2,3]{2,1,0:T(2,128)}, u32[]{:S(2)}) copy-start(s32[2,2,3]{2,1,0:T(2,128)} %param.13) | copy-start | bytes 148
  (60 other events, 611.9 us)
Sparse Core Ops, SparseCore 0:
  10.8 101.8 all-gather.10
  115.5 66.0 all-gather.12
  184.4 61.8 all-gather.8
  248.9 61.8 all-gather.14
  313.6 93.5 all-gather.16
  409.9 93.7 all-gather.18
  506.6 93.7 all-gather.20
  717.7 106.0 reduce-scatter.11
  829.3 106.2 reduce-scatter.9
  941.0 121.0 reduce-scatter.7
  1067.6 105.7 reduce-scatter.13
  1179.3 153.9 reduce-scatter.15
  1339.3 153.7 reduce-scatter.17
  1499.0 153.7 reduce-scatter.19
